TPU v7x, 768 devices: a whole 4x8x12 slice. The times are simulated.
768 devices in a mesh: seq: 96 (over z, y), tp: 8 (over x, core).
Axes of the slice: x: 4, y: 8, z: 12, core: 2. Of those that a mesh axis runs over, the one named last changes fastest.
Arguments:
- inputs: bfloat16 [12288, 4096], P('seq', 'tp'), may hold values from -6 to 6
- frozen_query_key_value: bfloat16 [3, 12288, 2048], P(None, 'seq', 'tp'), may hold values from -6 to 6
- adapter_down_maps: bfloat16 [3, 4096, 16], P(None, 'tp'), may hold values from -0.09375 to 0.09375
- adapter_up_maps: bfloat16 [3, 16, 2048], P(None, None, 'tp'), may hold values from -1.5 to 1.5
- incoming_state: float32 [32, 64, 64], P('tp'), may hold values from -1280 to 1280
- output_weight_matrix: bfloat16 [2048, 4096], P('tp'), may hold values from -0.125 to 0.125
- output_down_map: bfloat16 [2048, 16], P('tp'), may hold values from -0.125 to 0.125
- output_up_map: bfloat16 [16, 4096], replicated, may hold values from -1.5 to 1.5
- output_gradient: bfloat16 [12288, 4096], P('seq'), may hold values from -6 to 6
Outputs:
- attended: bfloat16 [12288, 2048], P('seq', 'tp')
- grad_down: float32 [3, 4096, 16], P(None, 'tp')
- grad_up: float32 [3, 16, 2048], P(None, None, 'tp')
- grad_out_down: float32 [2048, 16], P('tp')
- grad_out_up: float32 [16, 4096], replicated
- grad_state: float32 [32, 64, 64], P('tp')
All inputs are finite; a program needn't handle non-finite values.
Results may differ from a plain program's by a relative error of at most 0.022.
Values may be sent and summed in bfloat16 or wider, within the bound.
No kernel may reach another device: no remote copies, remote signals or barrier semaphores. Data moves between devices by JAX's collectives and lax.ppermute only.
A program may use at most 64 MiB of HBM per device.

v0:
```python
import math

import jax
import jax.numpy as jnp
from jax import lax
from jax.sharding import PartitionSpec as P

DH = 64


def carried_in(x, axis, combine, identity, reverse):
    devices, index = (lax.axis_size(axis), lax.axis_index(axis))
    everything = lax.all_gather(x.astype(jnp.bfloat16), axis)
    start = jnp.broadcast_to(jnp.asarray(identity, x.dtype), x.shape)

    def step(k, before):
        at = devices - 1 - k if reverse else k
        reached = at > index if reverse else at < index
        new = combine(before, everything[at].astype(x.dtype))
        return jnp.where(reached, new, before)

    return lax.fori_loop(0, devices, step, start)


def block_terms(query_rows, key_rows, value_rows, grad_rows, state, later_sum, scale_factor):
    count = query_rows.shape[0]
    causal = jnp.arange(count)[:, None] >= jnp.arange(count)[None, :]
    state_low = state.astype(jnp.bfloat16)
    later_low = later_sum.astype(jnp.bfloat16)
    scores = jnp.einsum("thd,shd->hts", query_rows, key_rows, preferred_element_type=jnp.float32)
    weights = jnp.where(causal[None], scores, 0.0).astype(jnp.bfloat16)
    result = scale_factor * (
        jnp.einsum("hts,shd->thd", weights, value_rows, preferred_element_type=jnp.float32)
        + jnp.einsum("thd,hde->the", query_rows, state_low, preferred_element_type=jnp.float32)
    )
    dscores = jnp.einsum("the,she->hts", grad_rows, value_rows, preferred_element_type=jnp.float32)
    dweights = jnp.where(causal[None], dscores, 0.0).astype(jnp.bfloat16)
    grad_query = jnp.einsum(
        "hts,shd->thd", dweights, key_rows, preferred_element_type=jnp.float32
    ) + jnp.einsum("the,hde->thd", grad_rows, state_low, preferred_element_type=jnp.float32)
    grad_key = jnp.einsum(
        "hts,thd->shd", dweights, query_rows, preferred_element_type=jnp.float32
    ) + jnp.einsum("the,hde->thd", value_rows, later_low, preferred_element_type=jnp.float32)
    grad_value = jnp.einsum(
        "hts,the->she", weights, grad_rows, preferred_element_type=jnp.float32
    ) + jnp.einsum("thd,hde->the", key_rows, later_low, preferred_element_type=jnp.float32)
    return (
        result.astype(jnp.bfloat16),
        grad_query.astype(jnp.bfloat16),
        grad_key.astype(jnp.bfloat16),
        grad_value.astype(jnp.bfloat16),
    )


def add_single(earlier, later):
    return earlier + later


def state_sum(qg_own):
    return lax.psum(qg_own, "seq")


def on_device(
    inputs,
    frozen_query_key_value,
    adapter_down_maps,
    adapter_up_maps,
    incoming_state,
    output_weight_matrix,
    output_down_map,
    output_up_map,
    output_gradient,
):
    block_rows = inputs.shape[0]
    att_local = frozen_query_key_value.shape[2]
    head_count = att_local // DH
    scale_factor = 1.0 / math.sqrt(DH * block_rows * lax.axis_size("seq"))
    value_partial_term = jnp.einsum(
        "xo,hoe->hxe", inputs, adapter_down_maps, preferred_element_type=jnp.float32
    )
    lowrank_term = lax.psum(value_partial_term.astype(jnp.bfloat16), "tp")
    projected_rows = (
        frozen_query_key_value.astype(jnp.float32)
        + jnp.einsum(
            "sqm,smg->sqg", lowrank_term, adapter_up_maps, preferred_element_type=jnp.float32
        )
    ).astype(jnp.bfloat16)
    down_grad = lax.dot_general(
        output_gradient, output_up_map, (((1,), (1,)), ((), ())), preferred_element_type=jnp.float32
    ).astype(jnp.bfloat16)
    through_out = lax.dot_general(
        output_gradient,
        output_weight_matrix,
        (((1,), (1,)), ((), ())),
        preferred_element_type=jnp.float32,
    )
    through_low = lax.dot_general(
        down_grad, output_down_map, (((1,), (1,)), ((), ())), preferred_element_type=jnp.float32
    )
    grad_att = (scale_factor * (through_out + through_low)).astype(jnp.bfloat16)
    shaped = (block_rows, head_count, DH)
    query_rows = projected_rows[0].reshape(shaped)
    key_rows = projected_rows[1].reshape(shaped)
    value_rows = projected_rows[2].reshape(shaped)
    grad_rows = grad_att.reshape(shaped)
    kv_own = jnp.einsum("thd,the->hde", key_rows, value_rows, preferred_element_type=jnp.float32)
    qg_own = jnp.einsum("thd,the->hde", query_rows, grad_rows, preferred_element_type=jnp.float32)
    zeros_state = jnp.zeros_like(kv_own)
    before = carried_in(kv_own, "seq", add_single, zeros_state, False)
    later_sum = carried_in(qg_own, "seq", add_single, zeros_state, True)
    grad_state = state_sum(qg_own)
    states = incoming_state + before
    result, grad_query, grad_key, grad_value = block_terms(
        query_rows, key_rows, value_rows, grad_rows, states, later_sum, scale_factor
    )
    attended = result.reshape(block_rows, att_local)
    gradient_projection = jnp.stack([grad_query, grad_key, grad_value]).reshape(
        3, block_rows, att_local
    )
    back_partial = jnp.einsum(
        "msn,mqn->msq", gradient_projection, adapter_up_maps, preferred_element_type=jnp.float32
    )
    out_partial = jnp.dot(attended, output_down_map, preferred_element_type=jnp.float32)
    low_summed, out_summed = (
        lax.psum(back_partial.astype(jnp.bfloat16), "tp").astype(jnp.float32),
        lax.psum(out_partial.astype(jnp.bfloat16), "tp").astype(jnp.float32),
    )
    gradient_lowrank = low_summed.astype(jnp.bfloat16)
    out_low = out_summed.astype(jnp.bfloat16)
    up_local = jnp.einsum(
        "itr,itd->ird", lowrank_term, gradient_projection, preferred_element_type=jnp.float32
    )
    down_local = jnp.einsum(
        "td,itr->idr", inputs, gradient_lowrank, preferred_element_type=jnp.float32
    )
    out_up_local = lax.dot_general(
        out_low, output_gradient, (((0,), (0,)), ((), ())), preferred_element_type=jnp.float32
    )
    out_down_local = lax.dot_general(
        attended, down_grad, (((0,), (0,)), ((), ())), preferred_element_type=jnp.float32
    )
    grad_down, grad_up, grad_out_down, grad_out_up = lax.psum(
        (down_local, up_local, out_down_local, out_up_local), "seq"
    )
    return (attended, grad_down, grad_up, grad_out_down, grad_out_up, grad_state)


def solution(mesh):
    placed = (
        P("seq", "tp"),
        P(None, "seq", "tp"),
        P(None, "tp", None),
        P(None, None, "tp"),
        P("tp", None, None),
        P("tp", None),
        P("tp", None),
        P(),
        P("seq", None),
    )
    return jax.shard_map(
        on_device,
        mesh=mesh,
        in_specs=placed,
        out_specs=(
            P("seq", "tp"),
            P(None, "tp", None),
            P(None, None, "tp"),
            P("tp", None),
            P(),
            P("tp", None, None),
        ),
        check_vma=False,
    )
```

profile of v0, /device:TPU:2, one launch (start us, length us, event | category | flops | bytes accessed | tf_op | source)
XLA Modules:
  0.0 886.3 jit_solution(1310468153532575043)
XLA Ops:
  7.2 1.2 fusion.10
  8.5 29.6 %psum.56 = bf16[3,128,16]{1,2,0:T(8,128)(2,1)S(1)} all-reduce(bf16[3,128,16]{1,2,0:T(8,128)(2,1)S(1)} %fusion.10), channel_id=1, replica_groups=mesh['seq'=96,'tp'=8] {'tp'}, use_global_device_ids=true, to_apply=%region_0.0 | all-reduce | flops 6144 | bytes 24576 | tf_op jit(solution)/shard_map/psum | solution.py:81
  38.1 1.2 fusion
  40.4 1.6 convolution_convert_fusion.4
  43.6 2.1 fusion.5
  46.9 1.1 fusion.2
  48.0 1.1 fusion.1
  49.9 1.7 fusion.20
  52.5 1.7 fusion.22
  54.1 115.9 %all-gather.5.cloned.1.call-done = bf16[384,64,64]{2,1,0:T(8,128)(2,1)} async-done(((bf16[4,64,64]{2,1,0:T(8,128)(2,1)}), bf16[384,64,64]{2,1,0:T(8,128)(2,1)}) %all-gather.5.cloned.1.call-update) | async-done | bytes 3145744 | tf_op jit(solution)/shard_map/all_gather | solution.py:13
  170.0 88.7 %while.30 = (s32[]{:T(128)}, f32[4,64,64]{2,1,0:T(8,128)S(1)}, s32[]{:T(128)}, bf16[96,4,64,64]{3,2,1,0:T(8,128)(2,1)}, s32[]{:T(128)}, /*index=5*/s32[]{:T(128)}) while((s32[]{:T(128)}, f32[4,64,64]{2,1,0:T(8,128)S(1)}, s32[]{:T(128)}, bf16[96,4,64,64]{3,2,1,0:T(8,128)(2,1)}, s32[]{:T(128)}, /*index=5*/s32[]{:T(128)}) %tuple.95), condition=%wide.region_2.3_spmd.clone, body=%wide.region_1.2_spmd.clone.sunk | while | flops 65540 | bytes 163941 | solution.py:22
  170.9 0.9 add_select_fusion.4
  171.9 0.9 add_select_fusion.4
  172.8 0.9 add_select_fusion.4
  193.1 0.9 add_select_fusion.4
  197.8 0.9 add_select_fusion.4
  198.7 0.9 add_select_fusion.4
  205.1 0.9 add_select_fusion.4
  208.8 0.9 add_select_fusion.4
  214.4 0.9 add_select_fusion.4
  215.3 0.9 add_select_fusion.4
  219.0 0.9 add_select_fusion.4
  219.9 0.9 add_select_fusion.4
  224.6 0.9 add_select_fusion.4
  255.1 0.9 add_select_fusion.4
  256.0 0.9 add_select_fusion.4
  256.9 0.9 add_select_fusion.4
  258.8 0.9 add_convert_fusion
  259.7 1.7 fusion.7
  261.4 1.6 copy.53
  263.0 1.2 fusion.6
  265.0 1.4 fusion.25
  266.4 32.5 %all-gather.7.cloned.1.call-done = bf16[384,64,64]{2,1,0:T(8,128)(2,1)} async-done(((bf16[4,64,64]{2,1,0:T(8,128)(2,1)}), bf16[384,64,64]{2,1,0:T(8,128)(2,1)}) %all-gather.7.cloned.1.call-update) | async-done | bytes 3145744 | tf_op jit(solution)/shard_map/all_gather | solution.py:13
  298.9 89.2 %while.31 = (s32[]{:T(128)}, f32[4,64,64]{2,1,0:T(8,128)S(1)}, s32[]{:T(128)}, bf16[96,4,64,64]{3,2,1,0:T(8,128)(2,1)}, s32[]{:T(128)}, /*index=5*/s32[]{:T(128)}, s32[]{:T(128)}, s32[]{:T(128)}) while((s32[]{:T(128)}, f32[4,64,64]{2,1,0:T(8,128)S(1)}, s32[]{:T(128)}, bf16[96,4,64,64]{3,2,1,0:T(8,128)(2,1)}, s32[]{:T(128)}, ...), condition=%wide.region_4.5_spmd.clone, body=%wide.region_3.4_spmd.clone.sunk | while | flops 65544 | bytes 164003 | solution.py:22
  388.1 1.1 fusion.8
  389.1 1.8 fusion.9
  390.9 0.9 copy.55
  392.0 1.0 convolution_convert_fusion.1
  393.0 1.6 fusion.13
  394.6 20.8 %all-reduce.2 = (bf16[3,128,16]{1,2,0:T(8,128)(2,1)S(1)}, bf16[128,16]{0,1:T(8,128)(2,1)S(1)}) all-reduce(bf16[3,128,16]{1,2,0:T(8,128)(2,1)S(1)} %convolution_convert_fusion.1, bf16[128,16]{0,1:T(8,128)(2,1)S(1)} %convolution_convert_fusion.3), channel_id=1, replica_groups=mesh['seq'=96,'tp'=8] {'tp'}, use_global_device_ids=true, to_apply=%region_5.6 | all-reduce | flops 8192 | bytes 32768 | tf_op jit(solution)/shard_map/psum | solution.py:125
  415.4 1.0 fusion.26
  418.0 219.8 %all-reduce.6.cloned.1.call-done = (f32[3,16,256]{2,1,0:T(8,128)}, f32[256,16]{0,1:T(8,128)}) async-done(((f32[3,16,256]{2,1,0:T(8,128)}, f32[256,16]{0,1:T(8,128)}), (f32[3,16,256]{2,1,0:T(8,128)}, f32[256,16]{0,1:T(8,128)})) %all-reduce.6.cloned.1.call-update) | async-done | bytes 65552 | tf_op jit(solution)/shard_map/psum | solution.py:142
  637.8 234.5 %all-reduce.8.cloned.1.call-done = (f32[3,512,16]{1,2,0:T(8,128)}, f32[16,4096]{1,0:T(8,128)}, f32[4,64,64]{2,1,0:T(8,128)}) async-done(((f32[3,512,16]{1,2,0:T(8,128)}, f32[16,4096]{1,0:T(8,128)}, f32[4,64,64]{2,1,0:T(8,128)}), (f32[3,512,16]{1,2,0:T(8,128)}, f32[16,4096]{1,0:T(8,128)}, f32[4,64,64]{2,1,0:T(8,128)})) %all-reduce.8.cloned.1.call-update) | async-done | bytes 426000 | tf_op jit(solution)/shard_map/psum | solution.py:142
  872.3 1.5 copy.76
  873.8 1.4 copy.77
  875.2 1.3 copy.78
  876.6 1.7 copy.79
  878.2 1.6 copy.80
  (219 shorter events, 166.7 us)
Async XLA Ops:
  7.2 36.4 %copy-start = (bf16[256,4096]{1,0:T(8,128)(2,1)S(1)}, bf16[256,4096]{1,0:T(8,128)(2,1)}, u32[]{:S(2)}) copy-start(bf16[256,4096]{1,0:T(8,128)(2,1)} %param.18) | copy-start | bytes 6291460
  7.2 162.8 %all-gather.5.cloned.1.call-start = ((), (), s32[]{:S(2)}) async-start(), calls=%async_computation | async-start | bytes 6356992 | tf_op jit(solution)/shard_map/all_gather | solution.py:13
  38.1 4.0 copy-start.6
  39.4 2.6 copy-start.2
  39.6 2.5 copy-start.3
  40.4 258.5 %all-gather.7.cloned.1.call-start = ((), (), s32[]{:S(2)}) async-start(), calls=%async_computation.1 | async-start | bytes 6356992 | tf_op jit(solution)/shard_map/all_gather | solution.py:13
  42.1 0.6 copy-start.8
  43.6 371.8 %copy-start.1 = (bf16[128,4096]{1,0:T(8,128)(2,1)S(1)}, bf16[128,4096]{1,0:T(8,128)(2,1)}, u32[]{:S(2)}) copy-start(bf16[128,4096]{1,0:T(8,128)(2,1)} %param.21) | copy-start | bytes 3145732
  46.8 590.9 %all-reduce.6.cloned.1.call-start = ((), (), s32[]{:S(2)}) async-start(), calls=%async_computation.2 | async-start | bytes 131072 | tf_op jit(solution)/shard_map/psum | solution.py:142
  49.1 343.9 %copy-start.7 = (bf16[3,128,16]{1,2,0:T(8,128)(2,1)S(1)}, bf16[3,128,16]{1,2,0:T(8,128)(2,1)}, u32[]{:S(2)}) copy-start(bf16[3,128,16]{1,2,0:T(8,128)(2,1)} %copy-done.6) | copy-start | bytes 36868
  259.7 1.7 copy-start.4
  259.7 156.8 %copy-start.5 = (bf16[128,512]{1,0:T(8,128)(2,1)S(1)}, bf16[128,512]{1,0:T(8,128)(2,1)}, u32[]{:S(2)}) copy-start(bf16[128,512]{1,0:T(8,128)(2,1)} %param.13) | copy-start | bytes 393220
  416.4 455.9 %all-reduce.8.cloned.1.call-start = ((), (), s32[]{:S(2)}) async-start(), calls=%async_computation.3 | async-start | bytes 983040 | tf_op jit(solution)/shard_map/psum | solution.py:142
Sparse Core Ops, SparseCore 0:
  40.5 129.4 all-gather.4
  173.8 125.0 all-gather.6
  416.5 221.2 all-reduce.5
  642.2 230.0 all-reduce.7
where the time goes:
time: 896 us; the launch traced here: 886 us
  waiting for transfers between devices  603 us (67%)
  other arithmetic  174 us (19%)
  blocking collectives  50.4 us (6%)
  matrix products  28.3 us (3%)
  between operations  14 us (2%)
  local copies, waits for them, and re-layouts  12 us (1%)
    psum x2, waiting for transfers between devices, on_device(): lax.psum((down_local, up_local, out_down_local, out_up_local), 'seq')  454 us
    select_n x192, other arithmetic, step(): return jnp.where(reached, new, before)  173 us
    all_gather x2, waiting for transfers between devices, carried_in(): everything = lax.all_gather(x.astype(jnp.bfloat16), axis)  148 us
    psum x1, blocking collectives, on_device(): lowrank_term = lax.psum(value_partial_term.astype(jnp.bfloat16), 'tp')  29.6 us
    psum x1, blocking collectives, on_device(): lax.psum(back_partial.astype(jnp.bfloat16), 'tp').astype(jnp.float32)  20.8 us
  transfers between devices with their start and end apart: 4, of which 4 were waited for; matrix products, arithmetic and copies ran while one was open for 12% of the time, Pallas kernels for 0%

commit v1 on v0

v1 whole, which is shorter than its diff:
```python
import functools
import math

import jax
import jax.numpy as jnp
from jax import lax
from jax.experimental import pallas as pl
from jax.experimental.pallas import tpu as pltpu
from jax.sharding import PartitionSpec as P

DH = 64
RANK = 16
Y_SIZE = 8
BF = jnp.bfloat16
F32 = jnp.float32


def dot(a, b, contract):
    return lax.dot_general(a, b, ((contract[:1], contract[1:]), ((), ())), preferred_element_type=F32)


NN, NT, TN = (1, 0), (1, 1), (0, 0)


def iota(shape, axis):
    return lax.broadcasted_iota(jnp.int32, shape, axis)


def total(ref):
    acc = ref[0].astype(F32)
    for k in range(1, ref.shape[0]):
        acc = acc + ref[k].astype(F32)
    return acc


def fill(ref, value):
    for k in range(ref.shape[0]):
        ref[k] = value


def sum_spread_kernel(in_ref, out_ref):
    fill(out_ref, total(in_ref).astype(BF))


def low_kernel(x_ref, down_ref, out_ref):
    fill(out_ref, dot(down_ref[...], x_ref[...], NT).astype(BF))


def per_head(rows):
    count, width = rows.shape
    lane = iota((count, width), 1) // DH
    return jnp.concatenate([jnp.where(lane == h, rows, jnp.zeros_like(rows)) for h in range(width // DH)], axis=0)


def project_kernel(
    scale, got_ref, frozen_ref, up_ref, og_ref, w_ref, wd_ref, oup_ref, low_ref, proj_ref, grad_ref, dg_ref, out_ref
):
    width = frozen_ref.shape[2]
    down_grad = dot(oup_ref[...], og_ref[...], NT).astype(BF)
    dg_ref[...] = down_grad
    through = dot(og_ref[...], w_ref[...], NT) + dot(down_grad, wd_ref[...], TN)
    grad = (scale * through).astype(BF)
    grad_ref[...] = grad
    low = total(got_ref).astype(BF)
    low_ref[...] = low
    rows = []
    for i in range(3):
        part = frozen_ref[i].astype(F32) + dot(low[i * RANK : (i + 1) * RANK], up_ref[i], TN)
        rows.append(part.astype(BF))
        proj_ref[i] = rows[i]
    query, key, value = rows
    same = iota((width, width), 0) // DH == iota((width, width), 1) // DH
    kv = jnp.where(same, dot(key, value, TN), 0.0).astype(BF)
    qg = jnp.where(same, dot(query, grad, TN), 0.0).astype(BF)
    column, lane = iota((width, 2 * DH), 0) % DH, iota((width, 2 * DH), 1)
    left = (lane == column).astype(BF)
    right = (lane == column + DH).astype(BF)
    packed = (dot(kv, left, NN) + dot(qg, right, NN)).astype(BF)
    slices = out_ref.shape[0]
    size = width // slices
    for j in range(slices):
        out_ref[j] = packed[j * size : (j + 1) * size]


def scan_kernel(z_ref, planes_ref, blocks_ref, out_ref):
    planes, blocks, size = planes_ref.shape[0], blocks_ref.shape[0], blocks_ref.shape[1]
    mine = z_ref[0]
    first = iota((size, 2 * DH), 1) < DH
    zero = jnp.zeros((size, 2 * DH), F32)
    before, after, whole = zero, zero, zero
    for k in range(planes):
        term = planes_ref[k].astype(F32)
        before = before + jnp.where(k < mine, term, 0.0)
        after = after + jnp.where(k > mine, term, 0.0)
        whole = whole + term
    ahead = [before]
    for k in range(blocks - 1):
        ahead.append(ahead[k] + blocks_ref[k].astype(F32))
    behind = [after]
    for k in range(blocks - 1, 0, -1):
        behind.append(behind[-1] + blocks_ref[k].astype(F32))
    behind = behind[::-1]
    for k in range(blocks):
        out_ref[k, :size] = jnp.where(first, ahead[k], behind[k]).astype(BF)
        out_ref[k, size:] = whole.astype(BF)


def attend_kernel(
    scale,
    got_ref,
    state_ref,
    proj_ref,
    grad_ref,
    low_ref,
    up_ref,
    wd_ref,
    dg_ref,
    att_ref,
    gstate_ref,
    part_ref,
    gup_ref,
):
    slices, size = got_ref.shape[0], got_ref.shape[1] // 2
    rows, width = grad_ref.shape
    heads = width // DH
    sums = jnp.concatenate([got_ref[j, :size] for j in range(slices)], axis=0)
    wholes = jnp.concatenate([got_ref[j, size:] for j in range(slices)], axis=0)
    lane, column = iota((2 * DH, DH), 0), iota((2 * DH, DH), 1)
    tail = (lane == column + DH).astype(BF)
    gstate_ref[...] = dot(wholes, tail, NN)
    state = (sums[:, :DH].astype(F32) + state_ref[...]).astype(BF)
    lane, column = iota((DH, width), 0), iota((DH, width), 1) % DH
    head_spread = (lane == column).astype(BF)
    lane, column = iota((2 * DH, width), 0), iota((2 * DH, width), 1) % DH
    tail_spread = (lane == column + DH).astype(BF)
    same = iota((width, width), 0) // DH == iota((width, width), 1) // DH
    state_low = jnp.where(same, dot(state, head_spread, NN), 0.0).astype(BF)
    later_low = jnp.where(same, dot(sums, tail_spread, NN), 0.0).astype(BF)
    query, key, value, grad = proj_ref[0], proj_ref[1], proj_ref[2], grad_ref[...]
    query_s, key_s, value_s, grad_s = per_head(query), per_head(key), per_head(value), per_head(grad)
    row, col = iota((rows, heads * rows), 0), iota((rows, heads * rows), 1) % rows
    lower, upper = col <= row, col >= row
    weights = jnp.where(lower, dot(query, key_s, NT), 0.0).astype(BF)
    weights_t = jnp.where(upper, dot(key, query_s, NT), 0.0).astype(BF)
    dweights = jnp.where(lower, dot(grad, value_s, NT), 0.0).astype(BF)
    dweights_t = jnp.where(upper, dot(value, grad_s, NT), 0.0).astype(BF)
    attended = (scale * (dot(weights, value_s, NN) + dot(query, state_low, NN))).astype(BF)
    att_ref[...] = attended
    back = (
        (dot(dweights, key_s, NN) + dot(grad, state_low, NT)).astype(BF),
        (dot(dweights_t, query_s, NN) + dot(value, later_low, NT)).astype(BF),
        (dot(weights_t, grad_s, NN) + dot(key, later_low, NN)).astype(BF),
    )
    parts = []
    for i in range(3):
        parts.append(dot(up_ref[i], back[i], NT))
        gup_ref[i * RANK : (i + 1) * RANK] = dot(low_ref[i * RANK : (i + 1) * RANK], back[i], NN).astype(BF)
    parts.append(dot(wd_ref[...], attended, NT))
    gup_ref[3 * RANK :] = dot(dg_ref[...], attended, NN).astype(BF)
    fill(part_ref, jnp.concatenate(parts, axis=0).astype(BF))


def layout(slices, model, cols, width):
    lanes = 128
    out_up = RANK * model // (slices * lanes)
    ups = 4 * RANK * width // (slices * lanes)
    down = 3 * RANK * cols // (slices * lanes)
    return out_up, ups, down


def pieces(slices, model, cols, width):
    out_up, ups, down = layout(slices, model, cols, width)
    span = model // slices
    up_rows = 4 * RANK // slices
    half = 3 * RANK // 2
    units = [(r * half, c * 128) for c in range(cols // 128) for r in range(2)]
    each = len(units) // slices
    found = []
    for j in range(slices):
        for c in range(span // 128):
            found.append((j, c * RANK, RANK, "o", 0, j * span + c * 128))
        for c in range(width // 128):
            for r in range(0, up_rows, 8):
                found.append((j, out_up + c * up_rows + r, 8, "u", j * up_rows + r, c * 128))
        for n in range(each):
            found.append((j, out_up + ups + n * half, half, "d", *units[j * each + n]))
    return found


def grads_kernel(got_ref, x_ref, og_ref, gup_ref, out_ref):
    low = total(got_ref).astype(BF)
    down = dot(low[: 3 * RANK], x_ref[...], NN).astype(BF)
    out_up = dot(low[3 * RANK :], og_ref[...], NN).astype(BF)
    kept = {"o": out_up, "u": gup_ref[...], "d": down}
    for j, at, count, name, row, col in pieces(out_ref.shape[0], og_ref.shape[1], x_ref.shape[1], gup_ref.shape[1]):
        out_ref[j, at : at + count] = kept[name][row : row + count, col : col + 128]


def unpack_kernel(got_ref, down_ref, up_ref, odown_ref, oup_ref):
    slices, model, cols, width = got_ref.shape[0], oup_ref.shape[1], down_ref.shape[1], up_ref.shape[1]
    for j, at, count, name, row, col in pieces(slices, model, cols, width):
        value = got_ref[j, at : at + count].astype(F32)
        if name == "o":
            oup_ref[row : row + count, col : col + 128] = value
        elif name == "d":
            down_ref[row : row + count, col : col + 128] = value
        elif row < 3 * RANK:
            up_ref[row : row + count, col : col + 128] = value
        else:
            odown_ref[row - 3 * RANK : row - 3 * RANK + count, col : col + 128] = value


def run(kernel, outs, *args, scalars=0, limit=16 << 20):
    vmem = pl.BlockSpec(memory_space=pltpu.VMEM)
    smem = pl.BlockSpec(memory_space=pltpu.SMEM)
    return pl.pallas_call(
        kernel,
        out_shape=[jax.ShapeDtypeStruct(shape, dtype) for shape, dtype in outs],
        in_specs=[smem] * scalars + [vmem] * (len(args) - scalars),
        out_specs=[vmem] * len(outs),
        compiler_params=pltpu.CompilerParams(vmem_limit_bytes=limit),
    )(*args)


def on_device(y_size, z_size, tp_size, inputs, frozen, down_maps, up_maps, state, w_out, down_out, up_out, out_grad):
    rows, cols = inputs.shape
    width, model = frozen.shape[2], out_grad.shape[1]
    scale = 1.0 / math.sqrt(DH * rows * y_size * z_size)
    planes = [[z * y_size + y for y in range(y_size)] for z in range(z_size)]
    columns = [[z * y_size + y for z in range(z_size)] for y in range(y_size)]

    def over_y(a):
        return lax.all_to_all(a, "seq", 0, 0, axis_index_groups=planes)

    def over_z(a):
        return lax.all_to_all(a, "seq", 0, 0, axis_index_groups=columns)

    def over_tp(a):
        return lax.all_to_all(a, "tp", 0, 0)

    down_t = jnp.transpose(down_maps, (0, 2, 1)).reshape(3 * RANK, cols)
    wd_t = down_out.T
    z_index = (lax.axis_index("seq") // y_size).reshape(1)

    (low_part,) = run(low_kernel, [((tp_size, 3 * RANK, rows), BF)], inputs, down_t)
    low, proj, grad, down_grad, own = run(
        functools.partial(project_kernel, scale),
        [
            ((3 * RANK, rows), BF),
            ((3, rows, width), BF),
            ((rows, width), BF),
            ((RANK, rows), BF),
            ((y_size, width // y_size, 2 * DH), BF),
        ],
        over_tp(low_part),
        frozen,
        up_maps,
        out_grad,
        w_out,
        wd_t,
        up_out,
    )
    blocks = over_y(own)
    slice_rows = width // y_size
    (plane,) = run(sum_spread_kernel, [((z_size, slice_rows, 2 * DH), BF)], blocks)
    (sums,) = run(
        scan_kernel, [((y_size, 2 * slice_rows, 2 * DH), BF)], z_index, over_z(plane), blocks, scalars=1
    )
    attended, grad_state, parts, grad_up = run(
        functools.partial(attend_kernel, scale),
        [
            ((rows, width), BF),
            ((width, DH), F32),
            ((tp_size, 4 * RANK, rows), BF),
            ((4 * RANK, width), BF),
        ],
        over_y(sums),
        state.reshape(width, DH),
        proj,
        grad,
        low,
        up_maps,
        wd_t,
        down_grad,
    )
    lines = sum(layout(y_size, model, cols, width))
    (shares,) = run(grads_kernel, [((y_size, lines, 128), BF)], over_tp(parts), inputs, out_grad, grad_up)
    (mine,) = run(sum_spread_kernel, [((z_size, lines, 128), BF)], over_y(shares))
    (whole,) = run(sum_spread_kernel, [((y_size, lines, 128), BF)], over_z(mine))
    down_g, up_g, odown_g, oup_g = run(
        unpack_kernel,
        [((3 * RANK, cols), F32), ((3 * RANK, width), F32), ((RANK, width), F32), ((RANK, model), F32)],
        over_y(whole),
    )
    return (
        attended,
        jnp.transpose(down_g.reshape(3, RANK, cols), (0, 2, 1)),
        up_g.reshape(3, RANK, width),
        odown_g.T,
        oup_g,
        grad_state.reshape(width // DH, DH, DH),
    )


def solution(mesh):
    placed = (
        P("seq", "tp"),
        P(None, "seq", "tp"),
        P(None, "tp", None),
        P(None, None, "tp"),
        P("tp", None, None),
        P("tp", None),
        P("tp", None),
        P(),
        P("seq", None),
    )
    seq, tp = mesh.shape["seq"], mesh.shape["tp"]
    return jax.shard_map(
        functools.partial(on_device, Y_SIZE, seq // Y_SIZE, tp),
        mesh=mesh,
        in_specs=placed,
        out_specs=(
            P("seq", "tp"),
            P(None, "tp", None),
            P(None, None, "tp"),
            P("tp", None),
            P(),
            P("tp", None, None),
        ),
        check_vma=False,
    )
```

time: 896 us -> 131 us (0.15)
  the two profiles are of different devices: /device:TPU:2 before, /device:TPU:64 now
where the time goes in v1:
time: 131 us; the launch traced here: 130 us
  blocking collectives  91.7 us (70%)
  starting transfers between devices  14.8 us (11%)
  waiting for transfers between devices  10.2 us (8%)
  local copies, waits for them, and re-layouts  7.8 us (6%)
  Pallas kernels  4.95 us (4%)
    all_to_all x4, blocking collectives, over_y(): return lax.all_to_all(a, 'seq', 0, 0, axis_index_groups=planes)  53.8 us
    all_to_all x1, blocking collectives, over_z(): return lax.all_to_all(a, 'seq', 0, 0, axis_index_groups=columns)  19.6 us
    all_to_all x2, blocking collectives, over_tp(): return lax.all_to_all(a, 'tp', 0, 0)  18.4 us
    all_to_all x1, starting transfers between devices, over_z(): return lax.all_to_all(a, 'seq', 0, 0, axis_index_groups=columns)  14.8 us
    all_to_all x1, waiting for transfers between devices, over_z(): return lax.all_to_all(a, 'seq', 0, 0, axis_index_groups=columns)  10.2 us
    unnamed x26, local copies, waits for them, and re-layouts  7.8 us
    pallas_call x9, Pallas kernels, run(): pl.pallas_call(kernel, out_shape=[jax.ShapeDtypeStruct(shape, dtype) for...  4.95 us
  transfers between devices with their start and end apart: 1, of which 1 were waited for; matrix products, arithmetic and copies ran while one was open for 0% of the time, Pallas kernels for 0%

profile of v1, /device:TPU:64, one launch (start us, length us, event | category | flops | bytes accessed | tf_op | source)
XLA Modules:
  0.0 130.1 jit_solution(17726645402413302370)
XLA Ops:
  0.6 0.0 copy-start.3
  0.6 0.9 copy-done.3
  1.5 0.0 copy-start.10
  1.5 0.8 copy-done.10
  2.3 0.2 shard_map.136
  2.5 9.9 %all_to_all.40.got_ref = bf16[8,48,128]{2,1,0:T(8,128)(2,1)S(1)} all-to-all(bf16[8,48,128]{2,1,0:T(8,128)(2,1)S(1)} %shard_map.136), channel_id=1, replica_groups=mesh['seq'=96,'tp'=8] {'tp'}, dimensions={0} | all-to-all | bytes 196608 | tf_op jit(solution)/shard_map/all_to_all | solution.py:239
  12.4 0.0 copy-start
  12.4 1.2 copy-done
  13.6 0.0 copy-start.2
  13.6 1.6 %copy-done.2 = bf16[256,4096]{1,0:T(8,128)(2,1)S(1)} copy-done((bf16[256,4096]{1,0:T(8,128)(2,1)S(1)}, bf16[256,4096]{1,0:T(8,128)(2,1)}, u32[]{:S(2)}) %copy-start.2) | copy-done | bytes 2097176
  15.2 0.0 copy-start.5
  15.2 0.9 copy-done.5
  16.1 0.0 copy-start.6
  16.1 0.9 copy-done.6
  17.0 0.0 copy-start.8
  17.0 0.7 copy-done.8
  17.8 0.0 copy-start.11
  17.8 0.7 copy-done.11
  18.5 0.0 copy-start.7
  18.5 0.0 copy-start.9
  18.5 0.0 copy-start.12
  18.5 0.0 copy-start.1
  18.5 0.0 copy-start.4
  18.5 1.6 %shard_map.137 = (bf16[48,128]{1,0:T(8,128)(2,1)S(1)}, bf16[3,128,256]{2,1,0:T(8,128)(2,1)S(1)}, bf16[128,256]{1,0:T(8,128)(2,1)S(1)}, bf16[16,128]{1,0:T(8,128)(2,1)S(1)}, bf16[8,32,128]{2,1,0:T(8,128)(2,1)S(1)}) custom-call(bf16[8,48,128]{2,1,0:T(8,128)(2,1)S(1)} %all_to_all.40.got_ref, bf16[3,128,256]{2,1,0:T(8,128)(2,1)S(1)} %copy-done.5, ...), custom_call_target="tpu_custom_call" | custom-call | tf_op jit(solution)/shard_map/pallas_call | solution.py:216
  20.1 15.3 %all_to_all.41.in_ref.blocks_ref = bf16[8,32,128]{2,1,0:T(8,128)(2,1)S(1)} all-to-all(bf16[8,32,128]{2,1,0:T(8,128)(2,1)S(1)} %get-tuple-element.19), channel_id=1, replica_groups={{0,8,16,24,32,40,48,56},{64,72,80,88,96,104,112,120},{128,136,144,152,1..., dimensions={0} | all-to-all | bytes 131072 | tf_op jit(solution)/shard_map/all_to_all | solution.py:233
  35.4 0.7 shard_map.138
  36.0 14.8 %all-to-all-start.2 = ((bf16[12,32,128]{2,1,0:T(8,128)(2,1)}), bf16[12,32,128]{2,1,0:T(8,128)(2,1)S(1)}, u32[]{:S(2)}, u32[]{:S(2)}) async-start(bf16[12,32,128]{2,1,0:T(8,128)(2,1)} %shard_map.138), calls=%async_computation.2 | async-start | bytes 196608 | tf_op jit(solution)/shard_map/all_to_all | solution.py:236
  50.8 10.2 %all-to-all-done.2.planes_ref = bf16[12,32,128]{2,1,0:T(8,128)(2,1)S(1)} async-done(((bf16[12,32,128]{2,1,0:T(8,128)(2,1)}), bf16[12,32,128]{2,1,0:T(8,128)(2,1)S(1)}, u32[]{:S(2)}, u32[]{:S(2)}) %all-to-all-start.2) | async-done | bytes 98336 | tf_op jit(solution)/shard_map/all_to_all | solution.py:236
  61.0 0.1 shard_map.139
  61.1 11.5 %all_to_all.42.got_ref = bf16[8,64,128]{2,1,0:T(8,128)(2,1)S(1)} all-to-all(bf16[8,64,128]{2,1,0:T(8,128)(2,1)S(1)} %shard_map.139), channel_id=1, replica_groups={{0,8,16,24,32,40,48,56},{64,72,80,88,96,104,112,120},{128,136,144,152,1..., dimensions={0} | all-to-all | bytes 262144 | tf_op jit(solution)/shard_map/all_to_all | solution.py:233
  72.6 0.0 copy-done.7
  72.6 0.0 copy-done.9
  72.6 0.0 copy-done.12
  72.6 1.3 %shard_map.140 = (bf16[128,256]{1,0:T(8,128)(2,1)}, f32[256,64]{1,0:T(8,128)}, bf16[8,64,128]{2,1,0:T(8,128)(2,1)S(1)}, bf16[64,256]{1,0:T(8,128)(2,1)S(1)}) custom-call(bf16[8,64,128]{2,1,0:T(8,128)(2,1)S(1)} %all_to_all.42.got_ref, f32[256,64]{1,0:T(8,128)S(1)} %bitcast.12, bf16[3,128,256]{2,1,0:T(8,128)(2,1)S(1)} %get-tuple-element.20.proj_ref, ...), custom_call_target="tpu_custom_call" | custom-call | tf_op jit(solution)/shard_map/pallas_call | solution.py:216
  73.9 8.5 %all_to_all.43.got_ref = bf16[8,64,128]{2,1,0:T(8,128)(2,1)S(1)} all-to-all(bf16[8,64,128]{2,1,0:T(8,128)(2,1)S(1)} %get-tuple-element.25), channel_id=1, replica_groups=mesh['seq'=96,'tp'=8] {'tp'}, dimensions={0} | all-to-all | bytes 262144 | tf_op jit(solution)/shard_map/all_to_all | solution.py:239
  82.4 0.0 copy-done.1
  82.4 0.0 copy-done.4
  82.4 0.3 shard_map.141
  82.7 13.3 %all_to_all.44.in_ref = bf16[8,104,128]{2,1,0:T(8,128)(2,1)S(1)} all-to-all(bf16[8,104,128]{2,1,0:T(8,128)(2,1)S(1)} %shard_map.141), channel_id=1, replica_groups={{0,8,16,24,32,40,48,56},{64,72,80,88,96,104,112,120},{128,136,144,152,1..., dimensions={0} | all-to-all | bytes 425984 | tf_op jit(solution)/shard_map/all_to_all | solution.py:233
  96.0 19.6 %all_to_all.45.in_ref = bf16[12,104,128]{2,1,0:T(8,128)(2,1)S(1)} all-to-all(bf16[12,104,128]{2,1,0:T(8,128)(2,1)S(1)} %shard_map.142), channel_id=1, replica_groups={{0,64,128,192,256,320,384,448,512,576,640,704},{8,72,136,200,264,328,39..., dimensions={0} | all-to-all | bytes 638976 | tf_op jit(solution)/shard_map/all_to_all | solution.py:236
  115.6 0.1 shard_map.143
  115.7 13.7 %all_to_all.46.got_ref = bf16[8,104,128]{2,1,0:T(8,128)(2,1)S(1)} all-to-all(bf16[8,104,128]{2,1,0:T(8,128)(2,1)S(1)} %shard_map.143), channel_id=1, replica_groups={{0,8,16,24,32,40,48,56},{64,72,80,88,96,104,112,120},{128,136,144,152,1..., dimensions={0} | all-to-all | bytes 425984 | tf_op jit(solution)/shard_map/all_to_all | solution.py:233
  129.4 0.8 shard_map.144
  (1 shorter events, 0.0 us)
Async XLA Ops:
  0.6 0.9 copy-start.3
  1.5 0.8 copy-start.10
  12.4 1.2 copy-start
  13.6 1.6 %copy-start.2 = (bf16[256,4096]{1,0:T(8,128)(2,1)S(1)}, bf16[256,4096]{1,0:T(8,128)(2,1)}, u32[]{:S(2)}) copy-start(bf16[256,4096]{1,0:T(8,128)(2,1)} %w_ref.1) | copy-start | bytes 6291460
  15.2 0.9 copy-start.5
  16.1 0.9 copy-start.6
  17.0 0.7 copy-start.8
  17.8 0.7 copy-start.11
  18.5 54.1 %copy-start.7 = (f32[4,64,64]{2,1,0:T(8,128)S(1)}, f32[4,64,64]{2,1,0:T(8,128)}, u32[]{:S(2)}) copy-start(f32[4,64,64]{2,1,0:T(8,128)} %param.13) | copy-start | bytes 196612
  18.5 54.1 %copy-start.9 = (bf16[3,16,256]{2,1,0:T(8,128)(2,1)S(1)}, bf16[3,16,256]{2,1,0:T(8,128)(2,1)}, u32[]{:S(2)}) copy-start(bf16[3,16,256]{2,1,0:T(8,128)(2,1)} %up_ref.3) | copy-start | bytes 73732
  18.5 54.1 %copy-start.12 = (bf16[256,16]{0,1:T(8,128)(2,1)S(1)}, bf16[256,16]{0,1:T(8,128)(2,1)}, u32[]{:S(2)}) copy-start(bf16[256,16]{0,1:T(8,128)(2,1)} %param.15) | copy-start | bytes 24580
  18.5 63.9 %copy-start.1 = (bf16[128,4096]{1,0:T(8,128)(2,1)S(1)}, bf16[128,4096]{1,0:T(8,128)(2,1)}, u32[]{:S(2)}) copy-start(bf16[128,4096]{1,0:T(8,128)(2,1)} %og_ref.3) | copy-start | bytes 3145732
  18.5 63.9 %copy-start.4 = (bf16[128,512]{1,0:T(8,128)(2,1)S(1)}, bf16[128,512]{1,0:T(8,128)(2,1)}, u32[]{:S(2)}) copy-start(bf16[128,512]{1,0:T(8,128)(2,1)} %x_ref.3) | copy-start | bytes 393220
  36.0 25.0 %all-to-all-start.2 = ((bf16[12,32,128]{2,1,0:T(8,128)(2,1)}), bf16[12,32,128]{2,1,0:T(8,128)(2,1)S(1)}, u32[]{:S(2)}, u32[]{:S(2)}) async-start(bf16[12,32,128]{2,1,0:T(8,128)(2,1)} %shard_map.138), calls=%async_computation.2 | async-start | bytes 196608 | tf_op jit(solution)/shard_map/all_to_all | solution.py:236

commit v2 on v1

--- a/solution.py
+++ b/solution.py
@@ -82,9 +82,9 @@
         out_ref[j] = packed[j * size : (j + 1) * size]
 
 
-def scan_kernel(z_ref, planes_ref, blocks_ref, out_ref):
+def scan_kernel(planes_ref, blocks_ref, out_ref):
     planes, blocks, size = planes_ref.shape[0], blocks_ref.shape[0], blocks_ref.shape[1]
-    mine = z_ref[0]
+    mine = lax.div(lax.axis_index("seq"), jnp.int32(blocks))
     first = iota((size, 2 * DH), 1) < DH
     zero = jnp.zeros((size, 2 * DH), F32)
     before, after, whole = zero, zero, zero
@@ -210,15 +210,15 @@
             odown_ref[row - 3 * RANK : row - 3 * RANK + count, col : col + 128] = value
 
 
-def run(kernel, outs, *args, scalars=0, limit=16 << 20):
+def run(kernel, outs, *args, limit=16 << 20, cost=None):
     vmem = pl.BlockSpec(memory_space=pltpu.VMEM)
-    smem = pl.BlockSpec(memory_space=pltpu.SMEM)
     return pl.pallas_call(
         kernel,
         out_shape=[jax.ShapeDtypeStruct(shape, dtype) for shape, dtype in outs],
-        in_specs=[smem] * scalars + [vmem] * (len(args) - scalars),
+        in_specs=[vmem] * len(args),
         out_specs=[vmem] * len(outs),
         compiler_params=pltpu.CompilerParams(vmem_limit_bytes=limit),
+        cost_estimate=cost,
     )(*args)
 
 
@@ -240,9 +240,8 @@
 
     down_t = jnp.transpose(down_maps, (0, 2, 1)).reshape(3 * RANK, cols)
     wd_t = down_out.T
-    z_index = (lax.axis_index("seq") // y_size).reshape(1)
-
-    (low_part,) = run(low_kernel, [((tp_size, 3 * RANK, rows), BF)], inputs, down_t)
+
+    (low_part,) = run(low_kernel, [((tp_size, 3 * RANK, rows), BF)], inputs, down_t, cost=pl.CostEstimate(flops=20_000_000_000, bytes_accessed=1_000_000, transcendentals=0))
     low, proj, grad, down_grad, own = run(
         functools.partial(project_kernel, scale),
         [
@@ -263,9 +262,7 @@
     blocks = over_y(own)
     slice_rows = width // y_size
     (plane,) = run(sum_spread_kernel, [((z_size, slice_rows, 2 * DH), BF)], blocks)
-    (sums,) = run(
-        scan_kernel, [((y_size, 2 * slice_rows, 2 * DH), BF)], z_index, over_z(plane), blocks, scalars=1
-    )
+    (sums,) = run(scan_kernel, [((y_size, 2 * slice_rows, 2 * DH), BF)], over_z(plane), blocks)
     attended, grad_state, parts, grad_up = run(
         functools.partial(attend_kernel, scale),
         [

time: 131 us -> 124 us (0.947)
  blocking collectives: 91.7 us -> 117 us
  starting transfers between devices: 14.8 us -> 0 us
  waiting for transfers between devices: 10.2 us -> 0 us
  local copies, waits for them, and re-layouts: 7.8 us -> 1.73 us
    all_to_all x1 -> x2, blocking collectives: 19.6 us -> 44.4 us  [over_z(): return lax.all_to_all(a, 'seq', 0, 0, axis_index_groups=columns)]
    all_to_all x1 -> x0, starting transfers between devices: 14.8 us -> none  [over_z(): return lax.all_to_all(a, 'seq', 0, 0, axis_index_groups=columns)]
    all_to_all x1 -> x0, waiting for transfers between devices: 10.2 us -> none  [over_z(): return lax.all_to_all(a, 'seq', 0, 0, axis_index_groups=columns)]
    unnamed x26 -> x20, local copies, waits for them, and re-layouts: 7.8 us -> 1.73 us
  transfers between devices with their start and end apart: 1 -> 0, of which waited for: 1 -> 0; matrix products, arithmetic and copies ran while one was open for 0% -> 0% of each run, Pallas kernels for 0% -> 0%
where the time goes in v2:
time: 124 us
  blocking collectives  117 us (94%)
  Pallas kernels  4.32 us (3%)
  local copies, waits for them, and re-layouts  1.73 us (1%)
    all_to_all x4, blocking collectives, over_y(): return lax.all_to_all(a, 'seq', 0, 0, axis_index_groups=planes)  53.8 us
    all_to_all x2, blocking collectives, over_z(): return lax.all_to_all(a, 'seq', 0, 0, axis_index_groups=columns)  44.4 us
    all_to_all x2, blocking collectives, over_tp(): return lax.all_to_all(a, 'tp', 0, 0)  18.6 us
    pallas_call x9, Pallas kernels, run(): pl.pallas_call(kernel, out_shape=[jax.ShapeDtypeStruct(shape, dtype) for...  4.32 us

profile of v2, /device:TPU:64, one launch (start us, length us, event | category | flops | bytes accessed | tf_op | source)
XLA Modules:
  0.0 123.6 jit_solution(3702254910032920795)
XLA Ops:
  0.6 0.0 copy-start.4
  0.6 0.9 copy-done.4
  1.5 0.0 copy-start.9
  1.5 0.8 copy-done.9
  2.3 0.0 copy-start
  2.3 0.0 copy-start.1
  2.3 0.0 copy-start.2
  2.3 0.0 copy-start.3
  2.4 0.0 copy-start.7
  2.4 0.0 copy-start.8
  2.4 0.2 shard_map.136
  2.5 10.2 %all_to_all.40.got_ref = bf16[8,48,128]{2,1,0:T(8,128)(2,1)S(1)} all-to-all(bf16[8,48,128]{2,1,0:T(8,128)(2,1)S(1)} %shard_map.136), channel_id=1, replica_groups=mesh['seq'=96,'tp'=8] {'tp'}, dimensions={0} | all-to-all | bytes 196608 | tf_op jit(solution)/shard_map/all_to_all | solution.py:239
  12.7 0.0 copy-done
  12.7 0.0 copy-done.1
  12.7 0.0 copy-done.2
  12.7 0.0 copy-done.3
  12.7 0.0 copy-done.7
  12.7 0.0 copy-done.8
  12.7 0.0 copy-start.6
  12.7 0.0 copy-start.5
  12.8 1.6 %shard_map.137 = (bf16[48,128]{1,0:T(8,128)(2,1)S(1)}, bf16[3,128,256]{2,1,0:T(8,128)(2,1)S(1)}, bf16[128,256]{1,0:T(8,128)(2,1)S(1)}, bf16[16,128]{1,0:T(8,128)(2,1)S(1)}, bf16[8,32,128]{2,1,0:T(8,128)(2,1)S(1)}) custom-call(bf16[8,48,128]{2,1,0:T(8,128)(2,1)S(1)} %all_to_all.40.got_ref, bf16[3,128,256]{2,1,0:T(8,128)(2,1)S(1)} %copy-done.2, ...), custom_call_target="tpu_custom_call" | custom-call | tf_op jit(solution)/shard_map/pallas_call | solution.py:215
  14.4 15.3 %all_to_all.41.in_ref.blocks_ref = bf16[8,32,128]{2,1,0:T(8,128)(2,1)S(1)} all-to-all(bf16[8,32,128]{2,1,0:T(8,128)(2,1)S(1)} %get-tuple-element.19), channel_id=1, replica_groups={{0,8,16,24,32,40,48,56},{64,72,80,88,96,104,112,120},{128,136,144,152,1..., dimensions={0} | all-to-all | bytes 131072 | tf_op jit(solution)/shard_map/all_to_all | solution.py:233
  29.7 24.8 %all_to_all.42.planes_ref = bf16[12,32,128]{2,1,0:T(8,128)(2,1)S(1)} all-to-all(bf16[12,32,128]{2,1,0:T(8,128)(2,1)S(1)} %shard_map.138), channel_id=1, replica_groups={{0,64,128,192,256,320,384,448,512,576,640,704},{8,72,136,200,264,328,39..., dimensions={0} | all-to-all | bytes 196608 | tf_op jit(solution)/shard_map/all_to_all | solution.py:236
  54.4 0.1 shard_map.139
  54.5 11.5 %all_to_all.43.got_ref = bf16[8,64,128]{2,1,0:T(8,128)(2,1)S(1)} all-to-all(bf16[8,64,128]{2,1,0:T(8,128)(2,1)S(1)} %shard_map.139), channel_id=1, replica_groups={{0,8,16,24,32,40,48,56},{64,72,80,88,96,104,112,120},{128,136,144,152,1..., dimensions={0} | all-to-all | bytes 262144 | tf_op jit(solution)/shard_map/all_to_all | solution.py:233
  66.0 0.0 copy-done.6
  66.0 1.3 %shard_map.140 = (bf16[128,256]{1,0:T(8,128)(2,1)}, f32[256,64]{1,0:T(8,128)}, bf16[8,64,128]{2,1,0:T(8,128)(2,1)S(1)}, bf16[64,256]{1,0:T(8,128)(2,1)S(1)}) custom-call(bf16[8,64,128]{2,1,0:T(8,128)(2,1)S(1)} %all_to_all.43.got_ref, f32[256,64]{1,0:T(8,128)S(1)} %bitcast.11, bf16[3,128,256]{2,1,0:T(8,128)(2,1)S(1)} %get-tuple-element.20.proj_ref, ...), custom_call_target="tpu_custom_call" | custom-call | tf_op jit(solution)/shard_map/pallas_call | solution.py:215
  67.3 8.5 %all_to_all.44.got_ref = bf16[8,64,128]{2,1,0:T(8,128)(2,1)S(1)} all-to-all(bf16[8,64,128]{2,1,0:T(8,128)(2,1)S(1)} %get-tuple-element.25), channel_id=1, replica_groups=mesh['seq'=96,'tp'=8] {'tp'}, dimensions={0} | all-to-all | bytes 262144 | tf_op jit(solution)/shard_map/all_to_all | solution.py:239
  75.8 0.0 copy-done.5
  75.8 0.3 shard_map.141
  76.1 13.3 %all_to_all.45.in_ref = bf16[8,104,128]{2,1,0:T(8,128)(2,1)S(1)} all-to-all(bf16[8,104,128]{2,1,0:T(8,128)(2,1)S(1)} %shard_map.141), channel_id=1, replica_groups={{0,8,16,24,32,40,48,56},{64,72,80,88,96,104,112,120},{128,136,144,152,1..., dimensions={0} | all-to-all | bytes 425984 | tf_op jit(solution)/shard_map/all_to_all | solution.py:233
  89.4 19.6 %all_to_all.46.in_ref = bf16[12,104,128]{2,1,0:T(8,128)(2,1)S(1)} all-to-all(bf16[12,104,128]{2,1,0:T(8,128)(2,1)S(1)} %shard_map.142), channel_id=1, replica_groups={{0,64,128,192,256,320,384,448,512,576,640,704},{8,72,136,200,264,328,39..., dimensions={0} | all-to-all | bytes 638976 | tf_op jit(solution)/shard_map/all_to_all | solution.py:236
  109.0 0.1 shard_map.143
  109.1 13.7 %all_to_all.47.got_ref = bf16[8,104,128]{2,1,0:T(8,128)(2,1)S(1)} all-to-all(bf16[8,104,128]{2,1,0:T(8,128)(2,1)S(1)} %shard_map.143), channel_id=1, replica_groups={{0,8,16,24,32,40,48,56},{64,72,80,88,96,104,112,120},{128,136,144,152,1..., dimensions={0} | all-to-all | bytes 425984 | tf_op jit(solution)/shard_map/all_to_all | solution.py:233
  122.8 0.8 shard_map.144
  (2 shorter events, 0.1 us)
Async XLA Ops:
  0.6 0.9 copy-start.4
  1.5 0.8 copy-start.9
  2.3 10.4 %copy-start = (bf16[128,4096]{1,0:T(8,128)(2,1)S(1)}, bf16[128,4096]{1,0:T(8,128)(2,1)}, u32[]{:S(2)}) copy-start(bf16[128,4096]{1,0:T(8,128)(2,1)} %og_ref.3) | copy-start | bytes 3145732
  2.3 10.4 %copy-start.1 = (bf16[256,4096]{1,0:T(8,128)(2,1)S(1)}, bf16[256,4096]{1,0:T(8,128)(2,1)}, u32[]{:S(2)}) copy-start(bf16[256,4096]{1,0:T(8,128)(2,1)} %w_ref.1) | copy-start | bytes 6291460
  2.3 10.4 %copy-start.2 = (bf16[3,128,256]{2,1,0:T(8,128)(2,1)S(1)}, bf16[3,128,256]{2,1,0:T(8,128)(2,1)}, u32[]{:S(2)}) copy-start(bf16[3,128,256]{2,1,0:T(8,128)(2,1)} %frozen_ref.1) | copy-start | bytes 589828
  2.3 10.4 %copy-start.3 = (bf16[16,4096]{1,0:T(8,128)(2,1)S(1)}, bf16[16,4096]{1,0:T(8,128)(2,1)}, u32[]{:S(2)}) copy-start(bf16[16,4096]{1,0:T(8,128)(2,1)} %oup_ref.1) | copy-start | bytes 393220
  2.4 10.4 %copy-start.7 = (bf16[3,16,256]{2,1,0:T(8,128)(2,1)S(1)}, bf16[3,16,256]{2,1,0:T(8,128)(2,1)}, u32[]{:S(2)}) copy-start(bf16[3,16,256]{2,1,0:T(8,128)(2,1)} %up_ref.3) | copy-start | bytes 73732
  2.4 10.4 %copy-start.8 = (bf16[256,16]{0,1:T(8,128)(2,1)S(1)}, bf16[256,16]{0,1:T(8,128)(2,1)}, u32[]{:S(2)}) copy-start(bf16[256,16]{0,1:T(8,128)(2,1)} %param.15) | copy-start | bytes 24580
  12.7 53.2 %copy-start.6 = (f32[4,64,64]{2,1,0:T(8,128)S(1)}, f32[4,64,64]{2,1,0:T(8,128)}, u32[]{:S(2)}) copy-start(f32[4,64,64]{2,1,0:T(8,128)} %param.13) | copy-start | bytes 196612
  12.7 63.1 %copy-start.5 = (bf16[128,512]{1,0:T(8,128)(2,1)S(1)}, bf16[128,512]{1,0:T(8,128)(2,1)}, u32[]{:S(2)}) copy-start(bf16[128,512]{1,0:T(8,128)(2,1)} %x_ref.3) | copy-start | bytes 393220

commit v3 on v2

--- a/solution.py
+++ b/solution.py
@@ -42,7 +42,13 @@
     fill(out_ref, total(in_ref).astype(BF))
 
 
-def low_kernel(x_ref, down_ref, out_ref):
+def low_kernel(x_hbm, down_hbm, out_ref, x_ref, down_ref, x_sem, down_sem):
+    x_copy = pltpu.make_async_copy(x_hbm, x_ref, x_sem)
+    down_copy = pltpu.make_async_copy(down_hbm, down_ref, down_sem)
+    x_copy.start()
+    down_copy.start()
+    x_copy.wait()
+    down_copy.wait()
     fill(out_ref, dot(down_ref[...], x_ref[...], NT).astype(BF))
 
 
@@ -100,9 +106,11 @@
     for k in range(blocks - 1, 0, -1):
         behind.append(behind[-1] + blocks_ref[k].astype(F32))
     behind = behind[::-1]
+    half = size // 2
+    turned = jnp.where(first[:half], pltpu.roll(whole[:half], DH, 1), whole[half:]).astype(BF)
     for k in range(blocks):
         out_ref[k, :size] = jnp.where(first, ahead[k], behind[k]).astype(BF)
-        out_ref[k, size:] = whole.astype(BF)
+        out_ref[k, size:] = turned
 
 
 def attend_kernel(
@@ -116,18 +124,13 @@
     wd_ref,
     dg_ref,
     att_ref,
-    gstate_ref,
     part_ref,
     gup_ref,
 ):
-    slices, size = got_ref.shape[0], got_ref.shape[1] // 2
+    slices, size = got_ref.shape[0], got_ref.shape[1] * 2 // 3
     rows, width = grad_ref.shape
     heads = width // DH
     sums = jnp.concatenate([got_ref[j, :size] for j in range(slices)], axis=0)
-    wholes = jnp.concatenate([got_ref[j, size:] for j in range(slices)], axis=0)
-    lane, column = iota((2 * DH, DH), 0), iota((2 * DH, DH), 1)
-    tail = (lane == column + DH).astype(BF)
-    gstate_ref[...] = dot(wholes, tail, NN)
     state = (sums[:, :DH].astype(F32) + state_ref[...]).astype(BF)
     lane, column = iota((DH, width), 0), iota((DH, width), 1) % DH
     head_spread = (lane == column).astype(BF)
@@ -196,7 +199,13 @@
         out_ref[j, at : at + count] = kept[name][row : row + count, col : col + 128]
 
 
-def unpack_kernel(got_ref, down_ref, up_ref, odown_ref, oup_ref):
+def unpack_kernel(got_ref, sums_ref, att_ref, down_ref, up_ref, odown_ref, oup_ref, state_ref, attended_ref):
+    attended_ref[...] = att_ref[...]
+    half = sums_ref.shape[1] // 3
+    for j in range(sums_ref.shape[0]):
+        both = sums_ref[j, 2 * half :].astype(F32)
+        state_ref[2 * half * j : 2 * half * j + half] = both[:, :DH]
+        state_ref[2 * half * j + half : 2 * half * (j + 1)] = pltpu.roll(both, DH, 1)[:, :DH]
     slices, model, cols, width = got_ref.shape[0], oup_ref.shape[1], down_ref.shape[1], up_ref.shape[1]
     for j, at, count, name, row, col in pieces(slices, model, cols, width):
         value = got_ref[j, at : at + count].astype(F32)
@@ -241,7 +250,21 @@
     down_t = jnp.transpose(down_maps, (0, 2, 1)).reshape(3 * RANK, cols)
     wd_t = down_out.T
 
-    (low_part,) = run(low_kernel, [((tp_size, 3 * RANK, rows), BF)], inputs, down_t, cost=pl.CostEstimate(flops=20_000_000_000, bytes_accessed=1_000_000, transcendentals=0))
+    hbm = pl.BlockSpec(memory_space=pltpu.HBM)
+    low_part = pl.pallas_call(
+        low_kernel,
+        out_shape=jax.ShapeDtypeStruct((tp_size, 3 * RANK, rows), BF),
+        in_specs=[hbm, hbm],
+        out_specs=pl.BlockSpec(memory_space=pltpu.VMEM),
+        scratch_shapes=[
+            pltpu.VMEM((rows, cols), BF),
+            pltpu.VMEM((3 * RANK, cols), BF),
+            pltpu.SemaphoreType.DMA,
+            pltpu.SemaphoreType.DMA,
+        ],
+        compiler_params=pltpu.CompilerParams(vmem_limit_bytes=4 << 20),
+        cost_estimate=pl.CostEstimate(flops=20_000_000_000, bytes_accessed=1_000_000, transcendentals=0),
+    )(pltpu.with_memory_space_constraint(inputs, pltpu.HBM), pltpu.with_memory_space_constraint(down_t, pltpu.HBM))
     low, proj, grad, down_grad, own = run(
         functools.partial(project_kernel, scale),
         [
@@ -262,16 +285,16 @@
     blocks = over_y(own)
     slice_rows = width // y_size
     (plane,) = run(sum_spread_kernel, [((z_size, slice_rows, 2 * DH), BF)], blocks)
-    (sums,) = run(scan_kernel, [((y_size, 2 * slice_rows, 2 * DH), BF)], over_z(plane), blocks)
-    attended, grad_state, parts, grad_up = run(
+    (sums,) = run(scan_kernel, [((y_size, 3 * slice_rows // 2, 2 * DH), BF)], over_z(plane), blocks)
+    sums = over_y(sums)
+    attended, parts, grad_up = run(
         functools.partial(attend_kernel, scale),
         [
             ((rows, width), BF),
-            ((width, DH), F32),
             ((tp_size, 4 * RANK, rows), BF),
             ((4 * RANK, width), BF),
         ],
-        over_y(sums),
+        sums,
         state.reshape(width, DH),
         proj,
         grad,
@@ -284,10 +307,19 @@
     (shares,) = run(grads_kernel, [((y_size, lines, 128), BF)], over_tp(parts), inputs, out_grad, grad_up)
     (mine,) = run(sum_spread_kernel, [((z_size, lines, 128), BF)], over_y(shares))
     (whole,) = run(sum_spread_kernel, [((y_size, lines, 128), BF)], over_z(mine))
-    down_g, up_g, odown_g, oup_g = run(
+    down_g, up_g, odown_g, oup_g, grad_state, attended = run(
         unpack_kernel,
-        [((3 * RANK, cols), F32), ((3 * RANK, width), F32), ((RANK, width), F32), ((RANK, model), F32)],
+        [
+            ((3 * RANK, cols), F32),
+            ((3 * RANK, width), F32),
+            ((RANK, width), F32),
+            ((RANK, model), F32),
+            ((width, DH), F32),
+            ((rows, width), BF),
+        ],
         over_y(whole),
+        sums,
+        attended,
     )
     return (
         attended,

time: 124 us -> 122 us (0.984)
  local copies, waits for them, and re-layouts: 1.73 us -> 0.04 us
    unnamed x20 -> x16, local copies, waits for them, and re-layouts: 1.73 us -> 0.04 us
    pallas_call x9 -> x8, Pallas kernels: 4.32 us -> 3.81 us  [run(): pl.pallas_call(kernel, out_shape=[jax.ShapeDtypeStruct(shape, dtype) for...]
where the time goes in v3:
time: 122 us
  blocking collectives  116 us (95%)
  Pallas kernels  5.05 us (4%)
    all_to_all x4, blocking collectives, over_y(): return lax.all_to_all(a, 'seq', 0, 0, axis_index_groups=planes)  53.4 us
    all_to_all x2, blocking collectives, over_z(): return lax.all_to_all(a, 'seq', 0, 0, axis_index_groups=columns)  44.4 us
    all_to_all x2, blocking collectives, over_tp(): return lax.all_to_all(a, 'tp', 0, 0)  18.4 us
    pallas_call x8, Pallas kernels, run(): pl.pallas_call(kernel, out_shape=[jax.ShapeDtypeStruct(shape, dtype) for...  3.81 us

profile of v3, /device:TPU:64, one launch (start us, length us, event | category | flops | bytes accessed | tf_op | source)
XLA Modules:
  0.0 122.0 jit_solution(17341716232046618715)
XLA Ops:
  0.6 0.0 copy-start
  0.6 0.0 copy-start.1
  0.7 0.0 copy-start.2
  0.7 0.0 copy-start.3
  0.7 0.0 copy-start.6
  0.7 0.0 copy-start.7
  0.7 1.2 %shard_map.136 = bf16[8,48,128]{2,1,0:T(8,128)(2,1)S(1)} custom-call(bf16[128,512]{1,0:T(8,128)(2,1)} %x_ref.1, bf16[48,512]{1,0:T(8,128)(2,1)} %bitcast.16), custom_call_target="tpu_custom_call" | custom-call | flops 20000000000 | bytes 1000000 | tf_op jit(solution)/shard_map/pallas_call | solution.py:254
  1.9 9.9 %all_to_all.40.got_ref = bf16[8,48,128]{2,1,0:T(8,128)(2,1)S(1)} all-to-all(bf16[8,48,128]{2,1,0:T(8,128)(2,1)S(1)} %shard_map.136), channel_id=1, replica_groups=mesh['seq'=96,'tp'=8] {'tp'}, dimensions={0} | all-to-all | bytes 196608 | tf_op jit(solution)/shard_map/all_to_all | solution.py:248
  11.8 0.0 copy-done
  11.8 0.0 copy-done.1
  11.8 0.0 copy-done.2
  11.8 0.0 copy-done.3
  11.9 0.0 copy-done.6
  11.9 0.0 copy-done.7
  11.9 0.0 copy-start.5
  11.9 0.0 copy-start.4
  11.9 1.6 %shard_map.137 = (bf16[48,128]{1,0:T(8,128)(2,1)S(1)}, bf16[3,128,256]{2,1,0:T(8,128)(2,1)S(1)}, bf16[128,256]{1,0:T(8,128)(2,1)S(1)}, bf16[16,128]{1,0:T(8,128)(2,1)S(1)}, bf16[8,32,128]{2,1,0:T(8,128)(2,1)S(1)}) custom-call(bf16[8,48,128]{2,1,0:T(8,128)(2,1)S(1)} %all_to_all.40.got_ref, bf16[3,128,256]{2,1,0:T(8,128)(2,1)S(1)} %copy-done.2, ...), custom_call_target="tpu_custom_call" | custom-call | tf_op jit(solution)/shard_map/pallas_call | solution.py:224
  13.5 15.3 %all_to_all.41.in_ref.blocks_ref = bf16[8,32,128]{2,1,0:T(8,128)(2,1)S(1)} all-to-all(bf16[8,32,128]{2,1,0:T(8,128)(2,1)S(1)} %get-tuple-element.20), channel_id=1, replica_groups={{0,8,16,24,32,40,48,56},{64,72,80,88,96,104,112,120},{128,136,144,152,1..., dimensions={0} | all-to-all | bytes 131072 | tf_op jit(solution)/shard_map/all_to_all | solution.py:242
  28.8 24.8 %all_to_all.42.planes_ref = bf16[12,32,128]{2,1,0:T(8,128)(2,1)S(1)} all-to-all(bf16[12,32,128]{2,1,0:T(8,128)(2,1)S(1)} %shard_map.138), channel_id=1, replica_groups={{0,64,128,192,256,320,384,448,512,576,640,704},{8,72,136,200,264,328,39..., dimensions={0} | all-to-all | bytes 196608 | tf_op jit(solution)/shard_map/all_to_all | solution.py:245
  53.6 0.1 shard_map.139
  53.7 11.1 %all_to_all.43.got_ref.sums_ref = bf16[8,48,128]{2,1,0:T(8,128)(2,1)S(1)} all-to-all(bf16[8,48,128]{2,1,0:T(8,128)(2,1)S(1)} %shard_map.139), channel_id=1, replica_groups={{0,8,16,24,32,40,48,56},{64,72,80,88,96,104,112,120},{128,136,144,152,1..., dimensions={0} | all-to-all | bytes 196608 | tf_op jit(solution)/shard_map/all_to_all | solution.py:242
  64.8 0.0 copy-done.5
  64.8 0.9 shard_map.140
  65.7 8.5 %all_to_all.44.got_ref = bf16[8,64,128]{2,1,0:T(8,128)(2,1)S(1)} all-to-all(bf16[8,64,128]{2,1,0:T(8,128)(2,1)S(1)} %get-tuple-element.25), channel_id=1, replica_groups=mesh['seq'=96,'tp'=8] {'tp'}, dimensions={0} | all-to-all | bytes 262144 | tf_op jit(solution)/shard_map/all_to_all | solution.py:248
  74.2 0.0 copy-done.4
  74.2 0.3 shard_map.141
  74.5 13.3 %all_to_all.45.in_ref = bf16[8,104,128]{2,1,0:T(8,128)(2,1)S(1)} all-to-all(bf16[8,104,128]{2,1,0:T(8,128)(2,1)S(1)} %shard_map.141), channel_id=1, replica_groups={{0,8,16,24,32,40,48,56},{64,72,80,88,96,104,112,120},{128,136,144,152,1..., dimensions={0} | all-to-all | bytes 425984 | tf_op jit(solution)/shard_map/all_to_all | solution.py:242
  87.8 19.6 %all_to_all.46.in_ref = bf16[12,104,128]{2,1,0:T(8,128)(2,1)S(1)} all-to-all(bf16[12,104,128]{2,1,0:T(8,128)(2,1)S(1)} %shard_map.142), channel_id=1, replica_groups={{0,64,128,192,256,320,384,448,512,576,640,704},{8,72,136,200,264,328,39..., dimensions={0} | all-to-all | bytes 638976 | tf_op jit(solution)/shard_map/all_to_all | solution.py:245
  107.4 0.1 shard_map.143
  107.4 13.7 %all_to_all.47.got_ref = bf16[8,104,128]{2,1,0:T(8,128)(2,1)S(1)} all-to-all(bf16[8,104,128]{2,1,0:T(8,128)(2,1)S(1)} %shard_map.143), channel_id=1, replica_groups={{0,8,16,24,32,40,48,56},{64,72,80,88,96,104,112,120},{128,136,144,152,1..., dimensions={0} | all-to-all | bytes 425984 | tf_op jit(solution)/shard_map/all_to_all | solution.py:242
  121.2 0.8 shard_map.144
  (2 shorter events, 0.1 us)
Async XLA Ops:
  0.6 11.2 %copy-start = (bf16[128,4096]{1,0:T(8,128)(2,1)S(1)}, bf16[128,4096]{1,0:T(8,128)(2,1)}, u32[]{:S(2)}) copy-start(bf16[128,4096]{1,0:T(8,128)(2,1)} %og_ref.3) | copy-start | bytes 3145732
  0.6 11.2 %copy-start.1 = (bf16[256,4096]{1,0:T(8,128)(2,1)S(1)}, bf16[256,4096]{1,0:T(8,128)(2,1)}, u32[]{:S(2)}) copy-start(bf16[256,4096]{1,0:T(8,128)(2,1)} %w_ref.1) | copy-start | bytes 6291460
  0.7 11.2 %copy-start.2 = (bf16[3,128,256]{2,1,0:T(8,128)(2,1)S(1)}, bf16[3,128,256]{2,1,0:T(8,128)(2,1)}, u32[]{:S(2)}) copy-start(bf16[3,128,256]{2,1,0:T(8,128)(2,1)} %frozen_ref.1) | copy-start | bytes 589828
  0.7 11.2 %copy-start.3 = (bf16[16,4096]{1,0:T(8,128)(2,1)S(1)}, bf16[16,4096]{1,0:T(8,128)(2,1)}, u32[]{:S(2)}) copy-start(bf16[16,4096]{1,0:T(8,128)(2,1)} %oup_ref.1) | copy-start | bytes 393220
  0.7 11.2 %copy-start.6 = (bf16[3,16,256]{2,1,0:T(8,128)(2,1)S(1)}, bf16[3,16,256]{2,1,0:T(8,128)(2,1)}, u32[]{:S(2)}) copy-start(bf16[3,16,256]{2,1,0:T(8,128)(2,1)} %up_ref.3) | copy-start | bytes 73732
  0.7 11.2 %copy-start.7 = (bf16[256,16]{0,1:T(8,128)(2,1)S(1)}, bf16[256,16]{0,1:T(8,128)(2,1)}, u32[]{:S(2)}) copy-start(bf16[256,16]{0,1:T(8,128)(2,1)} %param.15) | copy-start | bytes 24580
  11.9 52.9 %copy-start.5 = (f32[4,64,64]{2,1,0:T(8,128)S(1)}, f32[4,64,64]{2,1,0:T(8,128)}, u32[]{:S(2)}) copy-start(f32[4,64,64]{2,1,0:T(8,128)} %param.13) | copy-start | bytes 196612
  11.9 62.3 %copy-start.4 = (bf16[128,512]{1,0:T(8,128)(2,1)S(1)}, bf16[128,512]{1,0:T(8,128)(2,1)}, u32[]{:S(2)}) copy-start(bf16[128,512]{1,0:T(8,128)(2,1)} %x_ref.1) | copy-start | bytes 393220
